TPU v7x, 32 devices: a whole 2x2x4 slice. The times are simulated.
32 devices in a mesh: clip: 16 (over z, y, x), row: 2 (over core).
Axes of the slice: x: 2, y: 2, z: 4, core: 2. Of those that a mesh axis runs over, the one named last changes fastest.
Arguments:
- queries: bfloat16 [16, 512, 1792], P('clip', 'row'), may hold values from -36 to 36
- frames_kv: bfloat16 [16, 512, 512], P('clip', 'row'), may hold values from -20 to 20
- summary_kv: bfloat16 [16, 32, 512], P('clip', 'row'), may hold values from -6 to 6
- lengths: int32 [16], P('clip'), may hold values from 128 to 512, as said below
- caps: int32 [16], P('clip'), may hold values from 8 to 32, as said below
Outputs:
- attended: bfloat16 [16, 512, 1792], P('clip', 'row')
Inputs may be any that keep to these rules, and one draw needn't show every extreme that they name: `lengths`: some clip of every draw has 512 frame tokens. `caps`: some clip of every draw keeps 32 summary tokens.
All inputs are finite; a program needn't handle non-finite values.
Results may differ from a plain program's by a relative error of at most 0.01.
Values may be sent and summed in bfloat16 or wider, within the bound.
A program may use at most 64 MiB of HBM per device.

v0:
```python
import math

import jax
import jax.numpy as jnp
from jax import lax
from jax.sharding import PartitionSpec as P

KVH = 2
HD = 128
WINDOW = 128


masked_score = -1e30


def passed_along(block, axis, distance):
    devices = range(lax.axis_size(axis))
    route = [(i - distance, i) for i in devices if i - distance in devices]
    return lax.ppermute(block, axis, route)


def attend(state, query_heads, keys, values, valid):
    largest, total, accum = state
    scores = jnp.einsum(
        "tkgd,skd->kgts", query_heads, keys, preferred_element_type=jnp.float32
    ) * HD ** (-0.5)
    masked = jnp.where(valid, scores, masked_score)
    fresh = jnp.maximum(largest, jnp.max(masked, axis=-1))
    weights = jnp.where(valid, jnp.exp(masked - fresh[..., None]), 0.0)
    factor = jnp.exp(largest - fresh)
    total = total * factor + jnp.sum(weights, axis=-1)
    accum = accum * factor[..., None] + jnp.einsum(
        "kgts,skd->kgtd", weights.astype(jnp.bfloat16), values, preferred_element_type=jnp.float32
    )
    return (fresh, total, accum)


def split_rows(kv_rows):
    count = kv_rows.shape[0]
    keys = kv_rows[:, : KVH * HD].reshape(count, KVH, HD)
    values = kv_rows[:, KVH * HD :].reshape(count, KVH, HD)
    return (keys, values)


def fold_summary(state, piece, query_heads, clip_index):
    rows_kv, clip_caps = piece
    clip_count = rows_kv.shape[0]
    slot_count = rows_kv.shape[1]
    flat = rows_kv.reshape(clip_count * slot_count, rows_kv.shape[2])
    clip_ids = jnp.arange(clip_count)
    live = (jnp.arange(slot_count)[None, :] < clip_caps[:, None]) & (clip_ids[:, None] < clip_index)
    live = live.reshape(-1)
    count = clip_count * slot_count
    block = math.gcd(count, 512)
    blocks_kv = flat.reshape(count // block, block, flat.shape[1])
    blocks_live = live.reshape(count // block, block)

    def step_block(carry, item):
        kv_block, live_block = item
        keys, values = split_rows(kv_block)
        return (attend(carry, query_heads, keys, values, live_block), None)

    state, unused = lax.scan(step_block, state, (blocks_kv, blocks_live))
    return state


def shards(queries, frames_kv, summary_kv, lengths, caps):
    tokens_here = queries.shape[1]
    group = queries.shape[2] // (KVH * HD)
    row_index = lax.axis_index("row")
    clip_index = lax.axis_index("clip")
    own_heads = queries[0].reshape(tokens_here, KVH, group, HD)
    frames = frames_kv[0]
    rim = passed_along(frames[tokens_here - WINDOW :], "row", 1)
    local_kv = jnp.concatenate([rim, frames], axis=0)
    query_pos = row_index * tokens_here + jnp.arange(tokens_here)
    key_pos = row_index * tokens_here - WINDOW + jnp.arange(WINDOW + tokens_here)
    near = (
        (key_pos[None, :] >= 0)
        & (key_pos[None, :] <= query_pos[:, None])
        & (key_pos[None, :] > query_pos[:, None] - WINDOW)
    )
    start_state = (
        jnp.full((KVH, group, tokens_here), masked_score, jnp.float32),
        jnp.zeros((KVH, group, tokens_here), jnp.float32),
        jnp.zeros((KVH, group, tokens_here, HD), jnp.float32),
    )
    local_keys, local_values = split_rows(local_kv)
    state = attend(start_state, own_heads, local_keys, local_values, near)
    collected, every_cap = (
        lax.all_gather(summary_kv, "clip", axis=0, tiled=True),
        lax.all_gather(caps, "clip", axis=0, tiled=True),
    )
    state = fold_summary(
        state,
        (lax.all_gather(collected, "row", axis=1, tiled=True), every_cap),
        own_heads,
        clip_index,
    )
    largest, total, accum = state
    result = accum / total[..., None]
    result = jnp.transpose(result, (2, 0, 1, 3)).reshape(tokens_here, KVH * group * HD)
    result = jnp.where((query_pos < lengths[0])[:, None], result, 0.0)
    return result.astype(jnp.bfloat16)[None]


def solution(mesh):
    placed = (
        P("clip", "row", None),
        P("clip", "row", None),
        P("clip", "row", None),
        P("clip"),
        P("clip"),
    )
    return jax.shard_map(
        shards, mesh=mesh, in_specs=placed, out_specs=P("clip", "row", None), check_vma=False
    )
```

profile of v0, /device:TPU:28, one launch (start us, length us, event | category | flops | bytes accessed | tf_op | source)
XLA Modules:
  0.0 79.2 jit_solution(14224585013635414499)
XLA Ops:
  0.0 1.1 %copy.36 = bf16[1,256,512]{1,2,0:T(8,128)(2,1)S(1)} copy(bf16[1,256,512]{2,1,0:T(8,128)(2,1)} %param.6) | data formatting | bytes 524288 | tf_op args[1]
  1.1 1.7 %collective-permute-start = (bf16[128,512]{0,1:T(8,128)(2,1)S(1)}, bf16[128,512]{0,1:T(8,128)(2,1)S(1)}, u32[]{:S(2)}, u32[]{:S(2)}) collective-permute-start(bf16[128,512]{0,1:T(8,128)(2,1)S(1)} %slice_bitcast_fusion), channel_id=1, source_target_pairs={{0,1},{2,3},{4,5},{6,7},{8,9},{10,11},{12,13},{14,15},{16,17},{18,... | collective-permute-start | bytes 393224 | tf_op jit(solution)/shard_map/ppermute | solution.py:19
  2.9 36.1 %all_gather.10 = bf16[16,16,512]{2,1,0:T(8,128)(2,1)S(1)} all-gather(bf16[1,16,512]{2,1,0:T(8,128)(2,1)} %param.7), channel_id=1, replica_groups=mesh['clip'=16,'row'=2] {'clip'}, dimensions={0}, use_global_device_ids=true | all-gather | bytes 278528 | tf_op jit(solution)/shard_map/all_gather | solution.py:91
  39.0 2.2 %all_gather.11 = bf16[16,32,512]{2,1,0:T(8,128)(2,1)S(1)} all-gather(bf16[16,16,512]{2,1,0:T(8,128)(2,1)S(1)} %all_gather.10), channel_id=1, replica_groups=mesh['clip'=16,'row'=2] {'row'}, dimensions={1}, use_global_device_ids=true | all-gather | bytes 786432 | tf_op jit(solution)/shard_map/all_gather | solution.py:96
  41.8 1.2 %dynamic-slice = u32[1]{0:T(128)} dynamic-slice(u32[32]{0:T(128)} %constant.52, u32[]{:T(128)S(6)} %add.72), dynamic_slice_sizes={1} | dynamic-slice | bytes 12
  43.1 0.8 dynamic-update-slice
  43.8 16.8 %all-reduce = s32[16]{0:T(128)S(1)} all-reduce(s32[16]{0:T(128)S(1)} %dynamic-update-slice), channel_id=1, replica_groups=mesh['clip'=16,'row'=2] {'clip'}, use_global_device_ids=true, to_apply=%add | all-reduce | flops 16 | bytes 128
  60.7 0.1 fusion.23
  60.8 0.1 and.30
  60.8 0.1 copy.42
  61.0 1.5 %copy.38 = bf16[1,256,1792]{1,2,0:T(8,128)(2,1)S(1)} copy(bf16[1,256,1792]{2,1,0:T(8,128)(2,1)} %param.5) | data formatting | bytes 1835008 | tf_op args[0]
  62.5 4.3 %bitcast_reduce_fusion = (f32[2,7,256]{2,1,0:T(8,128)S(1)}, f32[2,512,256,7]{2,1,3,0:T(8,128)}) fusion(pred[512]{0:T(512)(128)(4,1)S(1)} %and.30, bf16[512,2,128,1]{0,2,3,1:T(8,128)(2,1)S(1)} %bitcast.95, bf16[256,2,7,128]{0,3,2,1:T(8,128)(2,1)S(1)} %bitcast.91), kind=kOutput, calls=%fused_computation.1 | convolution fusion | flops 475263488 | bytes 8534528 | tf_op jit(solution)/shard_map/while/body/eval_jaxpr/tkgd,skd->kgts/dot_general | solution.py:24
  66.7 0.2 compare_and_fusion
  66.9 0.1 copy.45
  67.0 0.0 copy-start
  67.9 0.0 collective-permute-done
  67.9 0.1 pad_maximum_fusion
  67.9 1.1 %fusion.4 = (f32[2,7,256]{2,1,0:T(8,128)S(1)}, f32[2,384,256,7]{2,1,3,0:T(8,128)S(1)}) fusion(pred[256,384]{0,1:T(8,128)(4,1)S(1)} %compare_and_fusion, bf16[384,2,128,1]{0,2,3,1:T(8,128)(2,1)S(1)} %bitcast.97, bf16[256,2,7,128]{0,3,2,1:T(8,128)(2,1)S(1)} %bitcast.92), kind=kOutput, calls=%fused_computation.9 | convolution fusion | flops 356446720 | bytes 6731776 | tf_op jit(solution)/shard_map/tkgd,skd->kgts/dot_general | solution.py:24
  69.0 1.1 %copy-done = f32[2,512,256,7]{2,1,3,0:T(8,128)S(1)} copy-done((f32[2,512,256,7]{2,1,3,0:T(8,128)S(1)}, f32[2,512,256,7]{2,1,3,0:T(8,128)}, u32[]{:S(2)}) %copy-start) | copy-done | bytes 7340056
  70.1 2.1 %fusion.2 = f32[2,7,256]{2,1,0:T(8,128)S(1)} fusion(f32[2,512,256,7]{2,1,3,0:T(8,128)S(1)} %copy-done, f32[2,7,256]{2,1,0:T(8,128)S(1)} %get-tuple-element.34, pred[512]{0:T(512)(128)(4,1)S(1)} %and.30), kind=kLoop, calls=%fused_computation.7 | loop fusion | flops 9171456 | bytes 7369216 | tf_op jit(solution)/shard_map/while/body/eval_jaxpr/reduce_sum | solution.py:31
  72.2 2.0 %fusion.7 = f32[2,7,256,128]{2,3,1,0:T(8,128)S(1)} fusion(bf16[512,2,128,1]{0,2,3,1:T(8,128)(2,1)S(1)} %bitcast.98, f32[2,512,256,7]{2,1,3,0:T(8,128)S(1)} %copy-done, f32[2,7,256]{2,1,0:T(8,128)S(1)} %get-tuple-element.34, pred[512]{0:T(512)(128)(4,1)S(1)} %and.30), kind=kOutput, calls=%fused_computation.12 | convolution fusion | flops 478937088 | bytes 9452032 | tf_op jit(solution)/shard_map/while/body/eval_jaxpr/kgts,skd->kgtd/dot_general | solution.py:32
  74.2 1.3 %fusion.5 = f32[2,7,256]{2,1,0:T(8,128)S(1)} fusion(f32[2,384,256,7]{2,1,3,0:T(8,128)S(1)} %get-tuple-element.36, f32[2,7,256]{2,1,0:T(8,128)S(1)} %get-tuple-element.33, pred[256,384]{0,1:T(8,128)(4,1)S(1)} %compare_and_fusion), kind=kLoop, calls=%fused_computation.10 | loop fusion | flops 6877696 | bytes 5632000 | tf_op jit(solution)/shard_map/reduce_sum | solution.py:31
  75.6 1.9 %fusion.14 = bf16[256,2,7,128]{0,3,2,1:T(8,128)(2,1)S(1)} fusion(f32[2,7,256,128]{2,3,1,0:T(8,128)S(1)} %fusion.7, bf16[384,2,128,1]{0,2,3,1:T(8,128)(2,1)S(1)} %bitcast.99, f32[2,384,256,7]{2,1,3,0:T(8,128)S(1)} %get-tuple-element.36, f32[2,7,256]{2,1,0:T(8,128)S(1)} %get-tuple-element.33, pred[256,384]{0,1:T(8,128)(4,1)S(1)} %compare_and_fusion, ...), kind=kOutput, calls=%fused_computation.18 | convolution fusion | flops 361496576 | bytes 8609792 | tf_op jit(solution)/shard_map/kgts,skd->kgtd/dot_general | solution.py:32
  77.5 0.6 copy.47
  78.1 1.1 %select_convert_fusion = bf16[1,256,1792]{2,1,0:T(8,128)(2,1)} fusion(bf16[1,256,1792]{2,1,0:T(8,128)(2,1)S(1)} %copy.47, pred[256]{0:T(512)(128)(4,1)S(1)} %fusion.25), kind=kLoop, calls=%fused_computation.21 | loop fusion | flops 458752 | bytes 1835264 | tf_op jit(solution)/shard_map/convert_element_type | solution.py:104
  (10 shorter events, 0.1 us)
Async XLA Ops:
  1.1 66.8 %collective-permute-start = (bf16[128,512]{0,1:T(8,128)(2,1)S(1)}, bf16[128,512]{0,1:T(8,128)(2,1)S(1)}, u32[]{:S(2)}, u32[]{:S(2)}) collective-permute-start(bf16[128,512]{0,1:T(8,128)(2,1)S(1)} %slice_bitcast_fusion), channel_id=1, source_target_pairs={{0,1},{2,3},{4,5},{6,7},{8,9},{10,11},{12,13},{14,15},{16,17},{18,... | collective-permute-start | bytes 393224 | tf_op jit(solution)/shard_map/ppermute | solution.py:19
  67.0 3.1 %copy-start = (f32[2,512,256,7]{2,1,3,0:T(8,128)S(1)}, f32[2,512,256,7]{2,1,3,0:T(8,128)}, u32[]{:S(2)}) copy-start(f32[2,512,256,7]{2,1,3,0:T(8,128)} %get-tuple-element.38) | copy-start | bytes 22020100
where the time goes:
time: 79.5 us; the launch traced here: 79.2 us
  blocking collectives  55.1 us (69%)
  matrix products  9.2 us (12%)
  local copies, waits for them, and re-layouts  6.69 us (8%)
  other arithmetic  4.89 us (6%)
  starting transfers between devices  1.75 us (2%)
  between operations  1.64 us (2%)
    all_gather x1, blocking collectives, shards(): lax.all_gather(summary_kv, 'clip', axis=0, tiled=True)  36.1 us
    unnamed x1, blocking collectives  16.8 us
    unnamed x7, local copies, waits for them, and re-layouts  5.66 us
    dot_general x2, matrix products, attend(): jnp.einsum('tkgd,skd->kgts', query_heads, keys, preferred_element_type=jn...  5.32 us
    dot_general x2, matrix products, attend(): jnp.einsum('kgts,skd->kgtd', weights.astype(jnp.bfloat16), values, prefer...  3.88 us
    reduce_sum x2, other arithmetic, attend(): total = total * factor + jnp.sum(weights, axis=-1)  3.38 us
    all_gather x1, blocking collectives, shards(): lax.all_gather(collected, 'row', axis=1, tiled=True)  2.17 us
    ppermute x1, starting transfers between devices, passed_along(): return lax.ppermute(block, axis, route)  1.75 us
  transfers between devices with their start and end apart: 1, of which 0 were waited for; matrix products, arithmetic and copies ran while one was open for 11% of the time, Pallas kernels for 0%

commit v1 on v0

v1 whole, which is shorter than its diff:
```python
import functools
import math

import jax
import jax.numpy as jnp
from jax import lax
from jax.experimental import pallas as pl
from jax.experimental.pallas import tpu as pltpu
from jax.sharding import PartitionSpec as P

KVH = 2
HD = 128
WINDOW = 128
MESH = pl.DeviceIdType.MESH
LOW = -1e30
DEAD = 1e30
EXP_SCALE = HD ** (-0.5) * math.log2(math.e)


def nt_dot(a, b):
    return lax.dot_general(a, b, (((1,), (1,)), ((), ())), preferred_element_type=jnp.float32)


def kernel(
    levels, group, heads,
    q_hbm, f_hbm, s_hbm, len_ref, cap_ref,
    out_ref,
    q, kv, raw, own, buf, acc, top,
    load_sem, a_send, a_recv, b_send, b_recv, c_send, c_recv, rim_send, rim_recv,
):
    tokens = q.shape[0]
    per_kv = heads // KVH
    half = own.shape[0]
    slots = 2 * half
    clip = lax.axis_index("clip")
    row = lax.axis_index("row")
    partner = 1 - row
    z = clip // group
    g = lax.rem(clip, group)
    blocks = tokens // WINDOW

    load_s = pltpu.make_async_copy(s_hbm, raw, load_sem.at[0])
    load_f = pltpu.make_async_copy(f_hbm, kv.at[pl.ds(WINDOW, tokens)], load_sem.at[1])
    load_q = pltpu.make_async_copy(q_hbm, q, load_sem.at[2])
    load_s.start()
    load_f.start()
    load_q.start()

    kw = KVH * HD
    buf[:, :, :, :kw] = jnp.zeros(buf.shape[:3] + (kw,), buf.dtype)
    buf[:, :, :, kw:] = jnp.full(buf.shape[:3] + (kw,), DEAD, buf.dtype)
    kv[:WINDOW] = jnp.zeros((WINDOW, kv.shape[1]), kv.dtype)

    barrier = pltpu.get_barrier_semaphore()
    pl.semaphore_signal(barrier, inc=1, device_id={"row": partner}, device_id_type=MESH)
    for zz in range(levels - 1):
        @pl.when(zz < z)
        def _():
            pl.semaphore_signal(barrier, inc=1, device_id={"clip": zz * group + g}, device_id_type=MESH)
    for gg in range(group):
        @pl.when((gg != g) & ((z > 0) | (gg < g)))
        def _():
            pl.semaphore_signal(barrier, inc=1, device_id={"clip": z * group + gg}, device_id_type=MESH)

    load_s.wait()
    slot_ids = row * half + lax.broadcasted_iota(jnp.int32, (half, kw), 0)
    own[:, :kw] = raw[:, :kw]
    own[:, kw:] = jnp.where(slot_ids < cap_ref[0], raw[:, kw:].astype(jnp.float32), DEAD).astype(own.dtype)

    count = 1 + (levels - 1 - z) + jnp.where(z > 0, group - 1, group - 1 - g)
    pl.semaphore_wait(barrier, count)

    def a_copy(src_z, dst_z):
        return pltpu.make_async_remote_copy(
            src_ref=own, dst_ref=buf.at[src_z * group + g, row],
            send_sem=a_send.at[dst_z], recv_sem=a_recv.at[src_z],
            device_id={"clip": dst_z * group + g}, device_id_type=MESH)

    def own_copy(gg):
        return pltpu.make_async_remote_copy(
            src_ref=own, dst_ref=buf.at[clip, row],
            send_sem=b_send.at[z * group + gg], recv_sem=b_recv.at[clip],
            device_id={"clip": z * group + gg}, device_id_type=MESH)

    def b_copy(p, gg):
        part = buf.at[p * group + g, row]
        return pltpu.make_async_remote_copy(
            src_ref=part, dst_ref=part,
            send_sem=b_send.at[p * group + gg], recv_sem=b_recv.at[p * group + g],
            device_id={"clip": z * group + gg}, device_id_type=MESH)

    def b_arrived(p, gg):
        part = buf.at[p * group + gg, row]
        pltpu.make_async_remote_copy(
            src_ref=part, dst_ref=part,
            send_sem=b_send.at[p * group + gg], recv_sem=b_recv.at[p * group + gg],
            device_id={"clip": z * group + gg}, device_id_type=MESH).wait_recv()

    def c_copy(p, side):
        part = buf.at[pl.ds(p * group, group), side]
        return pltpu.make_async_remote_copy(
            src_ref=part, dst_ref=part,
            send_sem=c_send.at[p], recv_sem=c_recv.at[p],
            device_id={"row": partner}, device_id_type=MESH)

    rim_copy = pltpu.make_async_remote_copy(
        src_ref=f_hbm.at[pl.ds(tokens - WINDOW, WINDOW)], dst_ref=kv.at[pl.ds(0, WINDOW)],
        send_sem=rim_send, recv_sem=rim_recv,
        device_id={"row": partner}, device_id_type=MESH)

    for zz in reversed(range(1, levels)):
        @pl.when(zz > z)
        def _():
            a_copy(z, zz).start()
    for gg in range(1, group):
        @pl.when(gg > g)
        def _():
            own_copy(gg).start()

    @pl.when(row == 0)
    def _():
        rim_copy.start()

    def stacked(k, j):
        rows = pl.ds(j * WINDOW, WINDOW)
        return jnp.concatenate(
            [q[rows, pl.ds((k * per_kv + i) * HD, HD)] for i in range(per_kv)], axis=0)

    ones = jnp.ones((2 * WINDOW, HD), jnp.bfloat16)

    def local(k, j):
        query = stacked(k, j)
        span = pl.ds(j * WINDOW, 2 * WINDOW)
        keys = kv[span, pl.ds(k * HD, HD)]
        values = jnp.concatenate([kv[span, pl.ds(kw + k * HD, HD)], ones], axis=1)
        t = lax.broadcasted_iota(jnp.int32, (WINDOW, 2 * WINDOW), 0)
        s = lax.broadcasted_iota(jnp.int32, (WINDOW, 2 * WINDOW), 1)
        near = (s > t) & (s <= t + WINDOW)
        if j == 0:
            near = near & (s >= jnp.where(row == 0, WINDOW, 0))
        bias = jnp.where(near, 0.0, LOW)
        scores = nt_dot(query, keys) + jnp.concatenate([bias] * per_kv, axis=0)
        largest = jnp.max(scores, axis=1, keepdims=True)
        weights = jnp.exp2((scores - largest) * EXP_SCALE).astype(jnp.bfloat16)
        unit = k * blocks + j
        acc[unit] = jnp.dot(weights, values, preferred_element_type=jnp.float32)
        top[unit] = jnp.broadcast_to(largest, top.shape[1:])

    load_f.wait()
    load_q.wait()
    for k in range(KVH):
        for j in range(1, blocks):
            local(k, j)

    for p in reversed(range(levels - 1)):
        @pl.when(p < z)
        def _():
            a_copy(p, z).wait_recv()
            for gg in range(group):
                @pl.when(gg != g)
                def _():
                    b_copy(p, gg).start()

    @pl.when(row == 1)
    def _():
        rim_copy.wait_recv()

    for k in range(KVH):
        local(k, 0)

    for p in reversed(range(levels)):
        @pl.when(p <= z)
        def _():
            for gg in range(group):
                @pl.when((gg != g) & ((p < z) | (gg < g)))
                def _():
                    b_arrived(p, gg)
            c_copy(p, row).start()

    for p in reversed(range(levels)):
        @pl.when(p <= z)
        def _():
            c_copy(p, partner).wait_recv()

    total = levels * group
    step = min(total, max(1, 512 // slots))
    first = (lax.broadcasted_iota(jnp.int32, (per_kv * WINDOW, HD), 1) == 0).astype(jnp.float32).astype(jnp.bfloat16)

    def remote(k, piece):
        part = pl.ds(piece * step, step)
        flat = (step * slots, HD)
        keys = buf[part, :, :, pl.ds(k * HD, HD)].reshape(flat)
        values = buf[part, :, :, pl.ds(kw + k * HD, HD)].reshape(flat).astype(jnp.float32)
        dead = values > 1e29
        keys = jnp.concatenate([keys, jnp.where(dead, LOW, 0.0).astype(jnp.bfloat16)], axis=1)
        values = jnp.where(dead, 0.0, values).astype(jnp.bfloat16)
        values = jnp.concatenate([values, jnp.ones(flat, jnp.bfloat16)], axis=1)
        for j in range(blocks):
            unit = k * blocks + j
            query = jnp.concatenate([stacked(k, j), first], axis=1)
            scores = nt_dot(query, keys)
            before = top[unit][:, :1]
            largest = jnp.maximum(before, jnp.max(scores, axis=1, keepdims=True))
            weights = jnp.exp2((scores - largest) * EXP_SCALE).astype(jnp.bfloat16)
            factor = jnp.exp2((before - largest) * EXP_SCALE)
            fresh = acc[unit] * factor + jnp.dot(weights, values, preferred_element_type=jnp.float32)
            acc[unit] = fresh
            if step < total:
                top[unit] = jnp.broadcast_to(largest, top.shape[1:])

    for k in range(KVH):
        if step == total:
            remote(k, 0)
        else:
            @pl.loop(0, total // step)
            def _(piece):
                remote(k, piece)
        for j in range(blocks):
            unit = k * blocks + j
            state = acc[unit]
            result = state[:, :HD] / state[:, HD:]
            pos = row * tokens + j * WINDOW + lax.broadcasted_iota(jnp.int32, (WINDOW, HD), 0)
            present = pos < len_ref[0]
            for i in range(per_kv):
                piece = result[i * WINDOW:(i + 1) * WINDOW]
                out_ref[pl.ds(j * WINDOW, WINDOW), pl.ds((k * per_kv + i) * HD, HD)] = (
                    jnp.where(present, piece, 0.0).astype(out_ref.dtype))

    for zz in range(1, levels):
        @pl.when(zz > z)
        def _():
            a_copy(z, zz).wait_send()
    for gg in range(1, group):
        @pl.when(gg > g)
        def _():
            own_copy(gg).wait_send()
    for p in range(levels - 1):
        @pl.when(p < z)
        def _():
            for gg in range(group):
                @pl.when(gg != g)
                def _():
                    b_copy(p, gg).wait_send()
    for p in range(levels):
        @pl.when(p <= z)
        def _():
            c_copy(p, row).wait_send()

    @pl.when(row == 0)
    def _():
        rim_copy.wait_send()


def shards(clips, queries, frames_kv, summary_kv, lengths, caps):
    tokens, width = queries.shape[1:]
    half, kv_width = summary_kv.shape[1:]
    heads = width // HD
    group = 1
    while group * group * 4 <= clips and clips % (group * 2) == 0:
        group *= 2
    levels = clips // group
    units = KVH * (tokens // WINDOW)
    rows = heads // KVH * WINDOW
    dma = pltpu.SemaphoreType.DMA
    anywhere = pl.BlockSpec(memory_space=pl.ANY)
    scalar = pl.BlockSpec(memory_space=pltpu.SMEM)
    out = pl.pallas_call(
        functools.partial(kernel, levels, group, heads),
        out_shape=jax.ShapeDtypeStruct((tokens, width), jnp.bfloat16),
        in_specs=[anywhere, anywhere, anywhere, scalar, scalar],
        out_specs=pl.BlockSpec(memory_space=pltpu.VMEM),
        scratch_shapes=[
            pltpu.VMEM((tokens, width), jnp.bfloat16),
            pltpu.VMEM((WINDOW + tokens, kv_width), jnp.bfloat16),
            pltpu.VMEM((half, kv_width), jnp.bfloat16),
            pltpu.VMEM((half, kv_width), jnp.bfloat16),
            pltpu.VMEM((clips, 2, half, kv_width), jnp.bfloat16),
            pltpu.VMEM((units, rows, 2 * HD), jnp.float32),
            pltpu.VMEM((units, rows, HD), jnp.float32),
            dma((3,)),
            dma((levels,)), dma((levels,)),
            dma((clips,)), dma((clips,)),
            dma((levels,)), dma((levels,)),
            dma, dma,
        ],
        compiler_params=pltpu.CompilerParams(
            collective_id=0, has_side_effects=True, vmem_limit_bytes=48 * 2**20),
    )(queries[0], frames_kv[0], summary_kv[0], lengths, caps)
    return out[None]


def solution(mesh):
    placed = (
        P("clip", "row", None),
        P("clip", "row", None),
        P("clip", "row", None),
        P("clip"),
        P("clip"),
    )
    return jax.shard_map(
        functools.partial(shards, mesh.shape["clip"]),
        mesh=mesh, in_specs=placed, out_specs=P("clip", "row", None), check_vma=False
    )
```

time: 79.5 us -> 22.9 us (0.29)
  the two profiles are of different devices: /device:TPU:28 before, /device:TPU:9 now
where the time goes in v1:
time: 22.9 us; the launch traced here: 22.7 us
  Pallas kernels  17.6 us (77%)
  local copies, waits for them, and re-layouts  3.76 us (16%)
  between operations  1.32 us (6%)
    pallas_call x1, Pallas kernels, shards(): pl.pallas_call(functools.partial(kernel, levels, group, heads), out_shape...  17.6 us
    unnamed x7, local copies, waits for them, and re-layouts  3.76 us

profile of v1, /device:TPU:9, one launch (start us, length us, event | category | flops | bytes accessed | tf_op | source)
XLA Modules:
  0.0 22.7 jit_solution(8613948226814242936)
XLA Ops:
  1.3 0.0 copy-start
  1.3 1.2 %copy-done = bf16[1,256,1792]{2,1,0:T(8,128)(2,1)S(1)} copy-done((bf16[1,256,1792]{2,1,0:T(8,128)(2,1)S(1)}, bf16[1,256,1792]{2,1,0:T(8,128)(2,1)}, u32[]{:S(2)}) %copy-start) | copy-done | bytes 917528
  2.5 0.0 copy-start.1
  2.5 0.9 %copy-done.1 = bf16[1,256,512]{2,1,0:T(8,128)(2,1)S(1)} copy-done((bf16[1,256,512]{2,1,0:T(8,128)(2,1)S(1)}, bf16[1,256,512]{2,1,0:T(8,128)(2,1)}, u32[]{:S(2)}) %copy-start.1) | copy-done | bytes 262168
  3.4 0.0 copy-start.2
  3.4 0.7 %copy-done.2 = bf16[1,16,512]{2,1,0:T(8,128)(2,1)S(1)} copy-done((bf16[1,16,512]{2,1,0:T(8,128)(2,1)S(1)}, bf16[1,16,512]{2,1,0:T(8,128)(2,1)}, u32[]{:S(2)}) %copy-start.2) | copy-done | bytes 16408
  4.1 17.6 %shard_map.55 = bf16[256,1792]{1,0:T(8,128)(2,1)S(1)} custom-call(bf16[256,1792]{1,0:T(8,128)(2,1)S(1)} %bitcast.5, bf16[256,512]{1,0:T(8,128)(2,1)S(1)} %bitcast.6, bf16[16,512]{1,0:T(8,128)(2,1)S(1)} %bitcast.7, s32[1]{0:T(128)S(6)} %copy.7.len_ref, s32[1]{0:T(128)S(6)} %copy.8.cap_ref), custom_call_target="tpu_custom_call" | custom-call | tf_op jit(solution)/shard_map/pallas_call | solution.py:267
  21.8 0.9 %copy.9 = bf16[1,256,1792]{2,1,0:T(8,128)(2,1)} copy(bf16[1,256,1792]{2,1,0:T(8,128)(2,1)S(1)} %bitcast.4) | data formatting | bytes 1835008
Async XLA Ops:
  1.3 1.2 %copy-start = (bf16[1,256,1792]{2,1,0:T(8,128)(2,1)S(1)}, bf16[1,256,1792]{2,1,0:T(8,128)(2,1)}, u32[]{:S(2)}) copy-start(bf16[1,256,1792]{2,1,0:T(8,128)(2,1)} %param.5) | copy-start | bytes 2752516
  2.5 0.9 %copy-start.1 = (bf16[1,256,512]{2,1,0:T(8,128)(2,1)S(1)}, bf16[1,256,512]{2,1,0:T(8,128)(2,1)}, u32[]{:S(2)}) copy-start(bf16[1,256,512]{2,1,0:T(8,128)(2,1)} %param.6) | copy-start | bytes 786436
  3.4 0.7 %copy-start.2 = (bf16[1,16,512]{2,1,0:T(8,128)(2,1)S(1)}, bf16[1,16,512]{2,1,0:T(8,128)(2,1)}, u32[]{:S(2)}) copy-start(bf16[1,16,512]{2,1,0:T(8,128)(2,1)} %param.7) | copy-start | bytes 49156

commit v2 on v1

--- a/solution.py
+++ b/solution.py
@@ -11,6 +11,7 @@
 KVH = 2
 HD = 128
 WINDOW = 128
+CHUNK = 32
 MESH = pl.DeviceIdType.MESH
 LOW = -1e30
 DEAD = 1e30
@@ -25,7 +26,7 @@
     levels, group, heads,
     q_hbm, f_hbm, s_hbm, len_ref, cap_ref,
     out_ref,
-    q, kv, raw, own, buf, acc, top,
+    q, kv, raw, own, buf, acc, top, scores, rounded, factor, near_bias,
     load_sem, a_send, a_recv, b_send, b_recv, c_send, c_recv, rim_send, rim_recv,
 ):
     tokens = q.shape[0]
@@ -126,25 +127,47 @@
         return jnp.concatenate(
             [q[rows, pl.ds((k * per_kv + i) * HD, HD)] for i in range(per_kv)], axis=0)
 
-    ones = jnp.ones((2 * WINDOW, HD), jnp.bfloat16)
+    rows = per_kv * WINDOW
+    wide = 2 * WINDOW
+    ones = jnp.ones((wide, HD), jnp.bfloat16)
+
+    def twice(x):
+        return jnp.concatenate([x, x], axis=1)
+
+    def attend(unit, query, keys, values, bias, start):
+        scores[unit] = nt_dot(query, keys)
+        for r in range(0, rows, CHUNK):
+            part = pl.ds(r, CHUNK)
+            s = scores[unit, part]
+            if bias is not None:
+                s = s + bias[pl.ds(r % WINDOW, CHUNK)]
+            largest = jnp.maximum(s[:, :HD], s[:, HD:])
+            largest = jnp.broadcast_to(jnp.max(largest, axis=1, keepdims=True), (CHUNK, HD))
+            if not start:
+                before = top[unit, part]
+                largest = jnp.maximum(before, largest)
+                factor[unit, part] = jnp.exp2((before - largest) * EXP_SCALE)
+            top[unit, part] = largest
+            rounded[unit, part] = jnp.exp2((s - twice(largest)) * EXP_SCALE).astype(jnp.bfloat16)
+        fresh = jnp.dot(rounded[unit], values, preferred_element_type=jnp.float32)
+        if start:
+            acc[unit] = fresh
+        else:
+            for r in range(0, rows, CHUNK):
+                part = pl.ds(r, CHUNK)
+                acc[unit, part] = acc[unit, part] * twice(factor[unit, part]) + fresh[r:r + CHUNK]
+
+    t = lax.broadcasted_iota(jnp.int32, (WINDOW, wide), 0)
+    s = lax.broadcasted_iota(jnp.int32, (WINDOW, wide), 1)
+    near = (s > t) & (s <= t + WINDOW)
+    near_bias[1] = jnp.where(near, 0.0, LOW)
+    near_bias[0] = jnp.where(near & (s >= jnp.where(row == 0, WINDOW, 0)), 0.0, LOW)
 
     def local(k, j):
-        query = stacked(k, j)
-        span = pl.ds(j * WINDOW, 2 * WINDOW)
+        span = pl.ds(j * WINDOW, wide)
         keys = kv[span, pl.ds(k * HD, HD)]
         values = jnp.concatenate([kv[span, pl.ds(kw + k * HD, HD)], ones], axis=1)
-        t = lax.broadcasted_iota(jnp.int32, (WINDOW, 2 * WINDOW), 0)
-        s = lax.broadcasted_iota(jnp.int32, (WINDOW, 2 * WINDOW), 1)
-        near = (s > t) & (s <= t + WINDOW)
-        if j == 0:
-            near = near & (s >= jnp.where(row == 0, WINDOW, 0))
-        bias = jnp.where(near, 0.0, LOW)
-        scores = nt_dot(query, keys) + jnp.concatenate([bias] * per_kv, axis=0)
-        largest = jnp.max(scores, axis=1, keepdims=True)
-        weights = jnp.exp2((scores - largest) * EXP_SCALE).astype(jnp.bfloat16)
-        unit = k * blocks + j
-        acc[unit] = jnp.dot(weights, values, preferred_element_type=jnp.float32)
-        top[unit] = jnp.broadcast_to(largest, top.shape[1:])
+        attend(k * blocks + j, stacked(k, j), keys, values, near_bias.at[min(j, 1)], True)
 
     load_f.wait()
     load_q.wait()
@@ -168,63 +191,60 @@
     for k in range(KVH):
         local(k, 0)
 
-    for p in reversed(range(levels)):
-        @pl.when(p <= z)
-        def _():
-            for gg in range(group):
-                @pl.when((gg != g) & ((p < z) | (gg < g)))
+    first = (lax.broadcasted_iota(jnp.int32, (rows, HD), 1) == 0).astype(jnp.float32).astype(jnp.bfloat16)
+    step = wide // slots
+    assert step % group == 0 or group % step == 0
+
+    def remote(piece):
+        part = pl.ds(piece * step, step)
+        for k in range(KVH):
+            keys = buf[part, :, :, pl.ds(k * HD, HD)].reshape(wide, HD)
+            values = buf[part, :, :, pl.ds(kw + k * HD, HD)].reshape(wide, HD).astype(jnp.float32)
+            dead = values > 1e29
+            keys = jnp.concatenate([keys, jnp.where(dead, LOW, 0.0).astype(jnp.bfloat16)], axis=1)
+            values = jnp.concatenate([jnp.where(dead, 0.0, values).astype(jnp.bfloat16), ones], axis=1)
+            for j in range(blocks):
+                query = jnp.concatenate([stacked(k, j), first], axis=1)
+                attend(k * blocks + j, query, keys, values, None, False)
+
+    per_piece = max(1, step // group)
+    for high in reversed(range(0, levels, per_piece)):
+        @pl.when(high <= z)
+        def _():
+            for p in reversed(range(high, min(high + per_piece, levels))):
+                @pl.when(p <= z)
                 def _():
-                    b_arrived(p, gg)
-            c_copy(p, row).start()
-
-    for p in reversed(range(levels)):
-        @pl.when(p <= z)
-        def _():
-            c_copy(p, partner).wait_recv()
-
-    total = levels * group
-    step = min(total, max(1, 512 // slots))
-    first = (lax.broadcasted_iota(jnp.int32, (per_kv * WINDOW, HD), 1) == 0).astype(jnp.float32).astype(jnp.bfloat16)
-
-    def remote(k, piece):
-        part = pl.ds(piece * step, step)
-        flat = (step * slots, HD)
-        keys = buf[part, :, :, pl.ds(k * HD, HD)].reshape(flat)
-        values = buf[part, :, :, pl.ds(kw + k * HD, HD)].reshape(flat).astype(jnp.float32)
-        dead = values > 1e29
-        keys = jnp.concatenate([keys, jnp.where(dead, LOW, 0.0).astype(jnp.bfloat16)], axis=1)
-        values = jnp.where(dead, 0.0, values).astype(jnp.bfloat16)
-        values = jnp.concatenate([values, jnp.ones(flat, jnp.bfloat16)], axis=1)
+                    for gg in range(group):
+                        @pl.when((gg != g) & ((p < z) | (gg < g)))
+                        def _():
+                            b_arrived(p, gg)
+                    c_copy(p, row).start()
+
+    for high in reversed(range(0, levels, per_piece)):
+        @pl.when(high <= z)
+        def _():
+            for p in reversed(range(high, min(high + per_piece, levels))):
+                @pl.when(p <= z)
+                def _():
+                    c_copy(p, partner).wait_recv()
+            pieces = max(1, group // step)
+            if pieces == 1:
+                remote(high // per_piece)
+            else:
+                @pl.loop(0, pieces)
+                def _(i):
+                    remote(high * pieces + i)
+
+    for k in range(KVH):
         for j in range(blocks):
             unit = k * blocks + j
-            query = jnp.concatenate([stacked(k, j), first], axis=1)
-            scores = nt_dot(query, keys)
-            before = top[unit][:, :1]
-            largest = jnp.maximum(before, jnp.max(scores, axis=1, keepdims=True))
-            weights = jnp.exp2((scores - largest) * EXP_SCALE).astype(jnp.bfloat16)
-            factor = jnp.exp2((before - largest) * EXP_SCALE)
-            fresh = acc[unit] * factor + jnp.dot(weights, values, preferred_element_type=jnp.float32)
-            acc[unit] = fresh
-            if step < total:
-                top[unit] = jnp.broadcast_to(largest, top.shape[1:])
-
-    for k in range(KVH):
-        if step == total:
-            remote(k, 0)
-        else:
-            @pl.loop(0, total // step)
-            def _(piece):
-                remote(k, piece)
-        for j in range(blocks):
-            unit = k * blocks + j
-            state = acc[unit]
-            result = state[:, :HD] / state[:, HD:]
             pos = row * tokens + j * WINDOW + lax.broadcasted_iota(jnp.int32, (WINDOW, HD), 0)
             present = pos < len_ref[0]
             for i in range(per_kv):
-                piece = result[i * WINDOW:(i + 1) * WINDOW]
+                part = pl.ds(i * WINDOW, WINDOW)
+                result = acc[unit, part, pl.ds(0, HD)] / acc[unit, part, pl.ds(HD, HD)]
                 out_ref[pl.ds(j * WINDOW, WINDOW), pl.ds((k * per_kv + i) * HD, HD)] = (
-                    jnp.where(present, piece, 0.0).astype(out_ref.dtype))
+                    jnp.where(present, result, 0.0).astype(out_ref.dtype))
 
     for zz in range(1, levels):
         @pl.when(zz > z)
@@ -277,6 +297,10 @@
             pltpu.VMEM((clips, 2, half, kv_width), jnp.bfloat16),
             pltpu.VMEM((units, rows, 2 * HD), jnp.float32),
             pltpu.VMEM((units, rows, HD), jnp.float32),
+            pltpu.VMEM((units, rows, 2 * WINDOW), jnp.float32),
+            pltpu.VMEM((units, rows, 2 * WINDOW), jnp.bfloat16),
+            pltpu.VMEM((units, rows, HD), jnp.float32),
+            pltpu.VMEM((2, WINDOW, 2 * WINDOW), jnp.float32),
             dma((3,)),
             dma((levels,)), dma((levels,)),
             dma((clips,)), dma((clips,)),
@@ -285,7 +309,7 @@
         ],
         compiler_params=pltpu.CompilerParams(
             collective_id=0, has_side_effects=True, vmem_limit_bytes=48 * 2**20),
-    )(queries[0], frames_kv[0], summary_kv[0], lengths, caps)
+    )(*[pltpu.with_memory_space_constraint(x[0], pltpu.HBM) for x in (queries, frames_kv, summary_kv)], lengths, caps)
     return out[None]
 
 

time: 22.9 us -> 16.6 us (0.72)
  Pallas kernels: 17.6 us -> 14.1 us
  local copies, waits for them, and re-layouts: 3.76 us -> 0.93 us
    pallas_call x1, Pallas kernels: 17.6 us -> 14.1 us  [shards(): pl.pallas_call(functools.partial(kernel, levels, group, heads), out_shape...]
    unnamed x7 -> x1, local copies, waits for them, and re-layouts: 3.76 us -> 0.93 us
where the time goes in v2:
time: 16.6 us; the launch traced here: 16.3 us
  Pallas kernels  14.1 us (85%)
  between operations  1.3 us (8%)
  local copies, waits for them, and re-layouts  0.93 us (6%)
    pallas_call x1, Pallas kernels, shards(): pl.pallas_call(functools.partial(kernel, levels, group, heads), out_shape...  14.1 us
    unnamed x1, local copies, waits for them, and re-layouts  0.93 us

profile of v2, /device:TPU:9, one launch (start us, length us, event | category | flops | bytes accessed | tf_op | source)
XLA Modules:
  0.0 16.3 jit_solution(4374361164906292471)
XLA Ops:
  1.3 14.1 %shard_map.55 = bf16[256,1792]{1,0:T(8,128)(2,1)S(1)} custom-call(bf16[256,1792]{1,0:T(8,128)(2,1)} %bitcast.5, bf16[256,512]{1,0:T(8,128)(2,1)} %bitcast.6, bf16[16,512]{1,0:T(8,128)(2,1)} %bitcast.7, s32[1]{0:T(128)S(6)} %copy.7.len_ref, s32[1]{0:T(128)S(6)} %copy.8.cap_ref), custom_call_target="tpu_custom_call" | custom-call | tf_op jit(solution)/shard_map/pallas_call | solution.py:287
  15.4 0.9 %copy.9 = bf16[1,256,1792]{2,1,0:T(8,128)(2,1)} copy(bf16[1,256,1792]{2,1,0:T(8,128)(2,1)S(1)} %bitcast.4) | data formatting | bytes 1835008

commit v3 on v2

--- a/solution.py
+++ b/solution.py
@@ -18,16 +18,24 @@
 EXP_SCALE = HD ** (-0.5) * math.log2(math.e)
 
 
+def each(low, high, act):
+    if high - low <= 4:
+        for i in range(low, high):
+            act(i)
+    else:
+        pl.loop(low, high)(act)
+
+
 def nt_dot(a, b):
     return lax.dot_general(a, b, (((1,), (1,)), ((), ())), preferred_element_type=jnp.float32)
 
 
 def kernel(
     levels, group, heads,
-    q_hbm, f_hbm, s_hbm, len_ref, cap_ref,
+    q_hbm, f_hbm, s_hbm, len_hbm, cap_hbm,
     out_ref,
-    q, kv, raw, own, buf, acc, top, scores, rounded, factor, near_bias,
-    load_sem, a_send, a_recv, b_send, b_recv, c_send, c_recv, rim_send, rim_recv,
+    len_ref, cap_ref, q, kv, raw, own, buf, acc, top, scores, rounded, factor, near_bias,
+    load_sem, up_send, up_recv, in_send, in_recv, rim_send, rim_recv,
 ):
     tokens = q.shape[0]
     per_kv = heads // KVH
@@ -43,7 +51,11 @@
     load_s = pltpu.make_async_copy(s_hbm, raw, load_sem.at[0])
     load_f = pltpu.make_async_copy(f_hbm, kv.at[pl.ds(WINDOW, tokens)], load_sem.at[1])
     load_q = pltpu.make_async_copy(q_hbm, q, load_sem.at[2])
+    load_len = pltpu.make_async_copy(len_hbm, len_ref, load_sem.at[3])
+    load_cap = pltpu.make_async_copy(cap_hbm, cap_ref, load_sem.at[4])
     load_s.start()
+    load_cap.start()
+    load_len.start()
     load_f.start()
     load_q.start()
 
@@ -54,69 +66,86 @@
 
     barrier = pltpu.get_barrier_semaphore()
     pl.semaphore_signal(barrier, inc=1, device_id={"row": partner}, device_id_type=MESH)
-    for zz in range(levels - 1):
-        @pl.when(zz < z)
-        def _():
-            pl.semaphore_signal(barrier, inc=1, device_id={"clip": zz * group + g}, device_id_type=MESH)
-    for gg in range(group):
+
+    @pl.when(z > 0)
+    def _():
+        pl.semaphore_signal(barrier, inc=1, device_id={"clip": clip - group}, device_id_type=MESH)
+    def greet(gg):
         @pl.when((gg != g) & ((z > 0) | (gg < g)))
         def _():
-            pl.semaphore_signal(barrier, inc=1, device_id={"clip": z * group + gg}, device_id_type=MESH)
+            for side in range(2):
+                pl.semaphore_signal(
+                    barrier, inc=1, device_id={"clip": z * group + gg, "row": side}, device_id_type=MESH)
+
+    each(0, group, greet)
 
     load_s.wait()
+    load_cap.wait()
     slot_ids = row * half + lax.broadcasted_iota(jnp.int32, (half, kw), 0)
     own[:, :kw] = raw[:, :kw]
     own[:, kw:] = jnp.where(slot_ids < cap_ref[0], raw[:, kw:].astype(jnp.float32), DEAD).astype(own.dtype)
 
-    count = 1 + (levels - 1 - z) + jnp.where(z > 0, group - 1, group - 1 - g)
-    pl.semaphore_wait(barrier, count)
-
-    def a_copy(src_z, dst_z):
+    above = jnp.where(z < levels - 1, 1, 0)
+    pl.semaphore_wait(barrier, 1 + above + 2 * jnp.where(z > 0, group - 1, group - 1 - g))
+
+    def up(src, p):
         return pltpu.make_async_remote_copy(
-            src_ref=own, dst_ref=buf.at[src_z * group + g, row],
-            send_sem=a_send.at[dst_z], recv_sem=a_recv.at[src_z],
-            device_id={"clip": dst_z * group + g}, device_id_type=MESH)
-
-    def own_copy(gg):
+            src_ref=src, dst_ref=buf.at[p * group + g, row],
+            send_sem=up_send.at[p], recv_sem=up_recv.at[p],
+            device_id={"clip": clip + group}, device_id_type=MESH)
+
+    def up_arrived(p):
+        part = buf.at[p * group + g, row]
+        pltpu.make_async_remote_copy(
+            src_ref=part, dst_ref=part, send_sem=up_send.at[p], recv_sem=up_recv.at[p],
+            device_id={"clip": clip - group}, device_id_type=MESH).wait_recv()
+
+    def across(src, p, gg, side):
+        block = p * group + g
         return pltpu.make_async_remote_copy(
-            src_ref=own, dst_ref=buf.at[clip, row],
-            send_sem=b_send.at[z * group + gg], recv_sem=b_recv.at[clip],
-            device_id={"clip": z * group + gg}, device_id_type=MESH)
-
-    def b_copy(p, gg):
-        part = buf.at[p * group + g, row]
-        return pltpu.make_async_remote_copy(
-            src_ref=part, dst_ref=part,
-            send_sem=b_send.at[p * group + gg], recv_sem=b_recv.at[p * group + g],
-            device_id={"clip": z * group + gg}, device_id_type=MESH)
-
-    def b_arrived(p, gg):
-        part = buf.at[p * group + gg, row]
+            src_ref=src, dst_ref=buf.at[block, row],
+            send_sem=in_send.at[p * group + gg, side], recv_sem=in_recv.at[block, row],
+            device_id={"clip": z * group + gg, "row": side}, device_id_type=MESH)
+
+    def across_arrived(p, gg, side):
+        part = buf.at[p * group + gg, side]
         pltpu.make_async_remote_copy(
             src_ref=part, dst_ref=part,
-            send_sem=b_send.at[p * group + gg], recv_sem=b_recv.at[p * group + gg],
-            device_id={"clip": z * group + gg}, device_id_type=MESH).wait_recv()
-
-    def c_copy(p, side):
-        part = buf.at[pl.ds(p * group, group), side]
-        return pltpu.make_async_remote_copy(
-            src_ref=part, dst_ref=part,
-            send_sem=c_send.at[p], recv_sem=c_recv.at[p],
-            device_id={"row": partner}, device_id_type=MESH)
+            send_sem=in_send.at[p * group + gg, side], recv_sem=in_recv.at[p * group + gg, side],
+            device_id={"row": partner}, device_id_type=MESH).wait_recv()
+
+    def forward(p):
+        part = buf.at[p * group + g, row]
+
+        @pl.when(z < levels - 1)
+        def _():
+            up(part, p).start()
+
+        def hand(gg):
+            @pl.when(gg != g)
+            def _():
+                for side in range(2):
+                    across(part, p, gg, side).start()
+
+        each(0, group, hand)
+        across(part, p, g, partner).start()
 
     rim_copy = pltpu.make_async_remote_copy(
         src_ref=f_hbm.at[pl.ds(tokens - WINDOW, WINDOW)], dst_ref=kv.at[pl.ds(0, WINDOW)],
         send_sem=rim_send, recv_sem=rim_recv,
         device_id={"row": partner}, device_id_type=MESH)
 
-    for zz in reversed(range(1, levels)):
-        @pl.when(zz > z)
-        def _():
-            a_copy(z, zz).start()
-    for gg in range(1, group):
+    @pl.when(z < levels - 1)
+    def _():
+        up(own, z).start()
+
+    def hand_own(gg):
         @pl.when(gg > g)
         def _():
-            own_copy(gg).start()
+            for side in range(2):
+                across(own, z, gg, side).start()
+
+    each(1, group, hand_own)
 
     @pl.when(row == 0)
     def _():
@@ -171,18 +200,18 @@
 
     load_f.wait()
     load_q.wait()
+    load_len.wait()
     for k in range(KVH):
         for j in range(1, blocks):
             local(k, j)
 
-    for p in reversed(range(levels - 1)):
-        @pl.when(p < z)
-        def _():
-            a_copy(p, z).wait_recv()
-            for gg in range(group):
-                @pl.when(gg != g)
-                def _():
-                    b_copy(p, gg).start()
+    def relay(back):
+        @pl.when(z >= back)
+        def _():
+            up_arrived(z - back)
+            forward(z - back)
+
+    relay(1)
 
     @pl.when(row == 1)
     def _():
@@ -191,9 +220,11 @@
     for k in range(KVH):
         local(k, 0)
 
+    each(2, levels, relay)
+
     first = (lax.broadcasted_iota(jnp.int32, (rows, HD), 1) == 0).astype(jnp.float32).astype(jnp.bfloat16)
     step = wide // slots
-    assert step % group == 0 or group % step == 0
+    assert slots * step == wide and (step % group == 0 or group % step == 0)
 
     def remote(piece):
         part = pl.ds(piece * step, step)
@@ -208,32 +239,39 @@
                 attend(k * blocks + j, query, keys, values, None, False)
 
     per_piece = max(1, step // group)
-    for high in reversed(range(0, levels, per_piece)):
+    assert levels % per_piece == 0
+    pieces = max(1, group // step)
+
+    def take(i):
+        high = (levels // per_piece - 1 - i) * per_piece
+
         @pl.when(high <= z)
         def _():
-            for p in reversed(range(high, min(high + per_piece, levels))):
+            def arrive(p):
                 @pl.when(p <= z)
                 def _():
-                    for gg in range(group):
+                    def block(gg):
                         @pl.when((gg != g) & ((p < z) | (gg < g)))
                         def _():
-                            b_arrived(p, gg)
-                    c_copy(p, row).start()
-
-    for high in reversed(range(0, levels, per_piece)):
-        @pl.when(high <= z)
-        def _():
-            for p in reversed(range(high, min(high + per_piece, levels))):
-                @pl.when(p <= z)
+                            for side in range(2):
+                                across_arrived(p, gg, side)
+
+                    each(0, group, block)
+
+                @pl.when(p < z)
                 def _():
-                    c_copy(p, partner).wait_recv()
-            pieces = max(1, group // step)
+                    across_arrived(p, g, partner)
+
+            for p in reversed(range(per_piece)):
+                arrive(high + p)
             if pieces == 1:
                 remote(high // per_piece)
             else:
                 @pl.loop(0, pieces)
                 def _(i):
                     remote(high * pieces + i)
+
+    each(0, levels // per_piece, take)
 
     for k in range(KVH):
         for j in range(blocks):
@@ -246,25 +284,37 @@
                 out_ref[pl.ds(j * WINDOW, WINDOW), pl.ds((k * per_kv + i) * HD, HD)] = (
                     jnp.where(present, result, 0.0).astype(out_ref.dtype))
 
-    for zz in range(1, levels):
-        @pl.when(zz > z)
-        def _():
-            a_copy(z, zz).wait_send()
-    for gg in range(1, group):
+    @pl.when(z < levels - 1)
+    def _():
+        up(own, z).wait_send()
+
+    def left_own(gg):
         @pl.when(gg > g)
         def _():
-            own_copy(gg).wait_send()
-    for p in range(levels - 1):
+            for side in range(2):
+                across(own, z, gg, side).wait_send()
+
+    each(1, group, left_own)
+
+    def left(p):
         @pl.when(p < z)
         def _():
-            for gg in range(group):
+            part = buf.at[p * group + g, row]
+
+            @pl.when(z < levels - 1)
+            def _():
+                up(part, p).wait_send()
+
+            def gone(gg):
                 @pl.when(gg != g)
                 def _():
-                    b_copy(p, gg).wait_send()
-    for p in range(levels):
-        @pl.when(p <= z)
-        def _():
-            c_copy(p, row).wait_send()
+                    for side in range(2):
+                        across(part, p, gg, side).wait_send()
+
+            each(0, group, gone)
+            across(part, p, g, partner).wait_send()
+
+    each(0, levels - 1, left)
 
     @pl.when(row == 0)
     def _():
@@ -283,13 +333,14 @@
     rows = heads // KVH * WINDOW
     dma = pltpu.SemaphoreType.DMA
     anywhere = pl.BlockSpec(memory_space=pl.ANY)
-    scalar = pl.BlockSpec(memory_space=pltpu.SMEM)
     out = pl.pallas_call(
         functools.partial(kernel, levels, group, heads),
         out_shape=jax.ShapeDtypeStruct((tokens, width), jnp.bfloat16),
-        in_specs=[anywhere, anywhere, anywhere, scalar, scalar],
+        in_specs=[anywhere] * 3 + [pl.BlockSpec(memory_space=pltpu.HBM)] * 2,
         out_specs=pl.BlockSpec(memory_space=pltpu.VMEM),
         scratch_shapes=[
+            pltpu.SMEM((1,), jnp.int32),
+            pltpu.SMEM((1,), jnp.int32),
             pltpu.VMEM((tokens, width), jnp.bfloat16),
             pltpu.VMEM((WINDOW + tokens, kv_width), jnp.bfloat16),
             pltpu.VMEM((half, kv_width), jnp.bfloat16),
@@ -301,15 +352,15 @@
             pltpu.VMEM((units, rows, 2 * WINDOW), jnp.bfloat16),
             pltpu.VMEM((units, rows, HD), jnp.float32),
             pltpu.VMEM((2, WINDOW, 2 * WINDOW), jnp.float32),
-            dma((3,)),
+            dma((5,)),
             dma((levels,)), dma((levels,)),
-            dma((clips,)), dma((clips,)),
-            dma((levels,)), dma((levels,)),
+            dma((clips, 2)), dma((clips, 2)),
             dma, dma,
         ],
         compiler_params=pltpu.CompilerParams(
             collective_id=0, has_side_effects=True, vmem_limit_bytes=48 * 2**20),
-    )(*[pltpu.with_memory_space_constraint(x[0], pltpu.HBM) for x in (queries, frames_kv, summary_kv)], lengths, caps)
+    )(*[pltpu.with_memory_space_constraint(x[0], pltpu.HBM)
+        for x in (queries, frames_kv, summary_kv)], lengths, caps)
     return out[None]
 
 

time: 16.6 us -> 17.7 us (1.066)
  the two profiles are of different devices: /device:TPU:9 before, /device:TPU:25 now
where the time goes in v3:
time: 17.7 us; the launch traced here: 17.4 us
  Pallas kernels  15.2 us (86%)
  between operations  1.3 us (7%)
  local copies, waits for them, and re-layouts  0.93 us (5%)
    pallas_call x1, Pallas kernels, shards(): pl.pallas_call(functools.partial(kernel, levels, group, heads), out_shape...  15.2 us
    unnamed x1, local copies, waits for them, and re-layouts  0.93 us

profile of v3, /device:TPU:25, one launch (start us, length us, event | category | flops | bytes accessed | tf_op | source)
XLA Modules:
  0.0 17.4 jit_solution(6993750322912084725)
XLA Ops:
  1.3 15.2 %shard_map.55 = bf16[256,1792]{1,0:T(8,128)(2,1)S(1)} custom-call(bf16[256,1792]{1,0:T(8,128)(2,1)} %bitcast.5, bf16[256,512]{1,0:T(8,128)(2,1)} %bitcast.6, bf16[16,512]{1,0:T(8,128)(2,1)} %bitcast.7, s32[1]{0:T(128)S(6)} %copy.7.len_hbm, s32[1]{0:T(128)S(6)} %copy.8.cap_hbm), custom_call_target="tpu_custom_call" | custom-call | tf_op jit(solution)/shard_map/pallas_call | solution.py:336
  16.5 0.9 %copy.9 = bf16[1,256,1792]{2,1,0:T(8,128)(2,1)} copy(bf16[1,256,1792]{2,1,0:T(8,128)(2,1)S(1)} %bitcast.4) | data formatting | bytes 1835008

commit v4 on v3

--- a/solution.py
+++ b/solution.py
@@ -67,9 +67,12 @@
     barrier = pltpu.get_barrier_semaphore()
     pl.semaphore_signal(barrier, inc=1, device_id={"row": partner}, device_id_type=MESH)
 
-    @pl.when(z > 0)
-    def _():
-        pl.semaphore_signal(barrier, inc=1, device_id={"clip": clip - group}, device_id_type=MESH)
+    def greet_below(zz):
+        @pl.when(zz < z)
+        def _():
+            pl.semaphore_signal(barrier, inc=1, device_id={"clip": zz * group + g}, device_id_type=MESH)
+
+    each(0, levels - 1, greet_below)
     def greet(gg):
         @pl.when((gg != g) & ((z > 0) | (gg < g)))
         def _():
@@ -85,20 +88,19 @@
     own[:, :kw] = raw[:, :kw]
     own[:, kw:] = jnp.where(slot_ids < cap_ref[0], raw[:, kw:].astype(jnp.float32), DEAD).astype(own.dtype)
 
-    above = jnp.where(z < levels - 1, 1, 0)
-    pl.semaphore_wait(barrier, 1 + above + 2 * jnp.where(z > 0, group - 1, group - 1 - g))
-
-    def up(src, p):
+    pl.semaphore_wait(barrier, levels - z + 2 * jnp.where(z > 0, group - 1, group - 1 - g))
+
+    def up(zz):
         return pltpu.make_async_remote_copy(
-            src_ref=src, dst_ref=buf.at[p * group + g, row],
-            send_sem=up_send.at[p], recv_sem=up_recv.at[p],
-            device_id={"clip": clip + group}, device_id_type=MESH)
+            src_ref=own, dst_ref=buf.at[clip, row],
+            send_sem=up_send.at[zz], recv_sem=up_recv.at[z],
+            device_id={"clip": zz * group + g}, device_id_type=MESH)
 
     def up_arrived(p):
         part = buf.at[p * group + g, row]
         pltpu.make_async_remote_copy(
             src_ref=part, dst_ref=part, send_sem=up_send.at[p], recv_sem=up_recv.at[p],
-            device_id={"clip": clip - group}, device_id_type=MESH).wait_recv()
+            device_id={"clip": p * group + g}, device_id_type=MESH).wait_recv()
 
     def across(src, p, gg, side):
         block = p * group + g
@@ -117,10 +119,6 @@
     def forward(p):
         part = buf.at[p * group + g, row]
 
-        @pl.when(z < levels - 1)
-        def _():
-            up(part, p).start()
-
         def hand(gg):
             @pl.when(gg != g)
             def _():
@@ -135,9 +133,14 @@
         send_sem=rim_send, recv_sem=rim_recv,
         device_id={"row": partner}, device_id_type=MESH)
 
-    @pl.when(z < levels - 1)
-    def _():
-        up(own, z).start()
+    def up_start(i):
+        zz = levels - 1 - i
+
+        @pl.when(zz > z)
+        def _():
+            up(zz).start()
+
+    each(0, levels - 1, up_start)
 
     def hand_own(gg):
         @pl.when(gg > g)
@@ -284,9 +287,12 @@
                 out_ref[pl.ds(j * WINDOW, WINDOW), pl.ds((k * per_kv + i) * HD, HD)] = (
                     jnp.where(present, result, 0.0).astype(out_ref.dtype))
 
-    @pl.when(z < levels - 1)
-    def _():
-        up(own, z).wait_send()
+    def up_left(zz):
+        @pl.when(zz > z)
+        def _():
+            up(zz).wait_send()
+
+    each(1, levels, up_left)
 
     def left_own(gg):
         @pl.when(gg > g)
@@ -300,10 +306,6 @@
         @pl.when(p < z)
         def _():
             part = buf.at[p * group + g, row]
-
-            @pl.when(z < levels - 1)
-            def _():
-                up(part, p).wait_send()
 
             def gone(gg):
                 @pl.when(gg != g)

time: 17.7 us -> 15.7 us (0.89)
  the two profiles are of different devices: /device:TPU:25 before, /device:TPU:9 now
where the time goes in v4:
time: 15.7 us; the launch traced here: 15.5 us
  Pallas kernels  13.2 us (84%)
  between operations  1.3 us (8%)
  local copies, waits for them, and re-layouts  0.93 us (6%)
    pallas_call x1, Pallas kernels, shards(): pl.pallas_call(functools.partial(kernel, levels, group, heads), out_shape...  13.2 us
    unnamed x1, local copies, waits for them, and re-layouts  0.93 us

profile of v4, /device:TPU:9, one launch (start us, length us, event | category | flops | bytes accessed | tf_op | source)
XLA Modules:
  0.0 15.5 jit_solution(4477297459755068054)
XLA Ops:
  1.3 13.2 %shard_map.55 = bf16[256,1792]{1,0:T(8,128)(2,1)S(1)} custom-call(bf16[256,1792]{1,0:T(8,128)(2,1)} %bitcast.5, bf16[256,512]{1,0:T(8,128)(2,1)} %bitcast.6, bf16[16,512]{1,0:T(8,128)(2,1)} %bitcast.7, s32[1]{0:T(128)S(6)} %copy.7.len_hbm, s32[1]{0:T(128)S(6)} %copy.8.cap_hbm), custom_call_target="tpu_custom_call" | custom-call | tf_op jit(solution)/shard_map/pallas_call | solution.py:338
  14.5 0.9 %copy.9 = bf16[1,256,1792]{2,1,0:T(8,128)(2,1)} copy(bf16[1,256,1792]{2,1,0:T(8,128)(2,1)S(1)} %bitcast.4) | data formatting | bytes 1835008
